TPU v7x, 128 devices: a whole 4x4x4 slice. The times are simulated.
128 devices in a mesh: pipe: 8 (over y, x_lo), seq: 16 (over z, x_hi, core).
Axes of the slice: x: 4 (x_hi: 2, x_lo: 2; x = x_hi * 2 + x_lo), y: 4, z: 4, core: 2. Of those that a mesh axis runs over, the one named last changes fastest.
Arguments:
- held: bfloat16 [8, 2048, 1536], P('pipe', 'seq'), may hold values from -6 to 6
- entering: bfloat16 [2048, 1536], P('seq'), may hold values from -6 to 6
- counts: int32 [9], replicated, may hold values from 1 to 256
- kind: int32 [8], P('pipe'), may hold values from 0 to 1
- modulation: float32 [8, 6, 1536], P('pipe'), may hold values from -4 to 4
- w_qkv: bfloat16 [8, 1536, 6144], P('pipe'), may hold values from -0.15625 to 0.15625
- w_out: bfloat16 [8, 2048, 1536], P('pipe'), may hold values from -0.125 to 0.125
- q_gain: float32 [8, 128], P('pipe'), may hold values from 1.5 to 6
- k_gain: float32 [8, 128], P('pipe'), may hold values from 1.5 to 6
Outputs:
- arrived: bfloat16 [2, 8, 2048, 1536], P(None, 'pipe', 'seq')
All inputs are finite; a program needn't handle non-finite values.
Results may differ from a plain program's by a relative error of at most 0.023.
The roundings to bfloat16 on the way count: a program that leaves them out, or rounds other values in their place, can miss the bound.
Values may be sent and summed in bfloat16 or wider, within the bound.
A program may use at most 128 MiB of HBM per device.

v0:
```python
import jax
import jax.numpy as jnp
from jax import lax
from jax.sharding import PartitionSpec as P

HD = 128
TXT = 256
eps = 1e-06


def from_behind(value, axis, steps):
    count = lax.axis_size(axis)
    pairs = [(source, (source + steps) % count) for source in range(count)]
    return lax.ppermute(value, axis, pairs)


def rms_heads(values_f32, gain):
    return (
        values_f32
        * lax.rsqrt(jnp.mean(values_f32 * values_f32, axis=-1, keepdims=True) + eps)
        * gain
    )


def shards(held, entering, counts, kind, modulation, w_qkv, w_out, q_gain, k_gain):
    section_id = lax.axis_index("pipe")
    seq_rank = lax.axis_index("seq")
    seq_devices = lax.axis_size("seq")
    tok_rows = held.shape[1]
    seq_total = tok_rows * seq_devices
    text_start = seq_total - TXT
    inner_width = w_out.shape[1]
    head_count = inner_width // HD
    section_count = counts.shape[0] - 1
    positions = seq_rank * tok_rows + jnp.arange(tok_rows, dtype=jnp.int32)
    params = modulation[0]
    choose = ((positions >= text_start) & (kind[0] == 0))[:, None]
    shift_row = jnp.where(choose, params[3], params[0])
    scale_row = jnp.where(choose, params[4], params[1])
    gate_row = jnp.where(choose, params[5], params[2])
    factor_scale = HD ** (-0.5)

    def pass_on(outcome):
        return from_behind(outcome, "pipe", 1)

    def run_block(resid, text_live):
        resid_f32 = resid.astype(jnp.float32)
        center = resid_f32 - jnp.mean(resid_f32, axis=-1, keepdims=True)
        normed = center * lax.rsqrt(jnp.mean(center * center, axis=-1, keepdims=True) + eps)
        mixed_in = (normed * (1.0 + scale_row) + shift_row).astype(jnp.bfloat16)
        projected = jnp.dot(mixed_in, w_qkv[0], preferred_element_type=jnp.float32)
        query_heads = rms_heads(
            projected[:, :inner_width].reshape(tok_rows, head_count, HD), q_gain[0]
        ).astype(jnp.bfloat16)
        key_heads = rms_heads(
            projected[:, inner_width : 2 * inner_width].reshape(tok_rows, head_count, HD), k_gain[0]
        ).astype(jnp.bfloat16)
        value_heads = (
            projected[:, 2 * inner_width :].reshape(tok_rows, head_count, HD).astype(jnp.bfloat16)
        )
        key_limit = text_start + text_live
        row_top = jnp.full((head_count, tok_rows), -1e30, jnp.float32)
        key_piece = lax.all_gather(key_heads, "seq", axis=0, tiled=True)
        value_piece = lax.all_gather(value_heads, "seq", axis=0, tiled=True)
        scores = (
            jnp.einsum("qhd,khd->hqk", query_heads, key_piece, preferred_element_type=jnp.float32)
            * factor_scale
        )
        key_pos = jnp.arange(key_piece.shape[0], dtype=jnp.int32)
        scores = jnp.where((key_pos < key_limit)[None, None, :], scores, -1e30)
        new_top = jnp.maximum(row_top, jnp.max(scores, axis=-1))
        weights = jnp.exp(scores - new_top[..., None])
        denom = jnp.sum(weights, axis=-1)
        accum = jnp.einsum(
            "hqk,khd->hqd",
            weights.astype(jnp.bfloat16),
            value_piece,
            preferred_element_type=jnp.float32,
        )
        row_top, denom, accum = (new_top, denom, accum)
        attended = (accum / denom[..., None]).astype(jnp.bfloat16).transpose(1, 0, 2)
        merged = attended.reshape(tok_rows, inner_width)
        update = jnp.dot(merged, w_out[0], preferred_element_type=jnp.float32)
        return (resid_f32 + gate_row * update).astype(jnp.bfloat16)

    outcome_one = run_block(held[0], counts[section_id])
    arrived_one = pass_on(outcome_one)
    inputs_two = jnp.where(section_id == 0, entering, arrived_one)
    outcome_two = run_block(inputs_two, counts[(section_id + section_count) % (section_count + 1)])
    arrived_two = pass_on(outcome_two)
    return jnp.stack([arrived_one, arrived_two])[:, None]


def solution(mesh):
    placed = (
        P("pipe", "seq", None),
        P("seq", None),
        P(),
        P("pipe"),
        P("pipe", None, None),
        P("pipe", None, None),
        P("pipe", None, None),
        P("pipe", None),
        P("pipe", None),
    )
    return jax.shard_map(
        shards, mesh=mesh, in_specs=placed, out_specs=P(None, "pipe", "seq", None), check_vma=False
    )
```

profile of v0, /device:TPU:1, one launch (start us, length us, event | category | flops | bytes accessed | tf_op | source)
XLA Modules:
  0.0 398.3 jit_solution(795105245037220855)
XLA Ops:
  10.6 8.1 %fusion.2 = f32[128,6144]{1,0:T(8,128)S(1)} fusion(bf16[1,1536,6144]{2,1,0:T(8,128)(2,1)} %param.14, bf16[1,128,1536]{2,1,0:T(8,128)(2,1)} %param.9, f32[1536]{0:T(1024)S(1)} %get-tuple-element.9, f32[1536]{0:T(1024)S(1)} %get-tuple-element.10, f32[1536]{0:T(1024)S(1)} %get-tuple-element.6, f32[1536]{0:T(1024)S(1)} %get-tuple-element.7, ...), kind=kOutput, calls=%fused_computation.2 | convolution fusion | flops 2417688576 | bytes 22439040 | tf_op jit(solution)/shard_map/dot_general | solution.py:51
  18.7 1.6 slice_bitcast_fusion.1
  21.0 2.4 fusion.51
  24.3 2.0 copy.58
  26.4 1.4 copy.61
  30.0 70.0 %all-gather.5.cloned.1.call-done = bf16[2048,16,128]{2,0,1:T(8,128)(2,1)} async-done(((bf16[128,16,128]{2,0,1:T(8,128)(2,1)}), bf16[2048,16,128]{2,0,1:T(8,128)(2,1)}) %all-gather.5.cloned.1.call-update) | async-done | bytes 8388624 | tf_op jit(solution)/shard_map/all_gather | solution.py:63
  100.0 12.1 %fusion.4 = (f32[16,128]{1,0:T(8,128)S(1)}, f32[16,128,2048]{2,1,0:T(8,128)}) fusion(pred[2048]{0:T(1024)(128)(4,1)S(1)} %iota_compare_fusion.1, bf16[2048,16,128]{2,0,1:T(8,128)(2,1)} %all-gather.5.cloned.1.call-done, bf16[128,16,128]{2,1,0:T(8,128)(2,1)S(1)} %multiply_convert_fusion.2), kind=kOutput, calls=%fused_computation.8 | convolution fusion | flops 1086322688 | bytes 25700352 | tf_op jit(solution)/shard_map/qhd,khd->hqk/dot_general | solution.py:66
  112.1 7.9 %fusion.6 = f32[16,128]{1,0:T(8,128)S(1)} fusion(f32[16,128,2048]{2,1,0:T(8,128)} %get-tuple-element.21, f32[16,128]{1,0:T(8,128)S(1)} %broadcast_maximum_fusion.1, pred[2048]{0:T(1024)(128)(4,1)S(1)} %iota_compare_fusion.1), kind=kLoop, calls=%fused_computation.10 | loop fusion | flops 16775168 | bytes 16795648 | tf_op jit(solution)/shard_map/reduce_sum | solution.py:73
  120.0 56.6 %all-gather.7.cloned.1.call-done = bf16[2048,16,128]{0,2,1:T(8,128)(2,1)} async-done(((bf16[128,16,128]{0,2,1:T(8,128)(2,1)}), bf16[2048,16,128]{0,2,1:T(8,128)(2,1)}) %all-gather.7.cloned.1.call-update) | async-done | bytes 8388624 | tf_op jit(solution)/shard_map/all_gather | solution.py:64
  176.6 10.7 %divide_convert_fusion.1 = bf16[128,16,128]{0,2,1:T(8,128)(2,1)S(1)} fusion(bf16[2048,16,128]{0,2,1:T(8,128)(2,1)} %all-gather.7.cloned.1.call-done, f32[16,128,2048]{2,1,0:T(8,128)} %get-tuple-element.21, f32[16,128]{1,0:T(8,128)S(1)} %broadcast_maximum_fusion.1, pred[2048]{0:T(1024)(128)(4,1)S(1)} %iota_compare_fusion.1, f32[128,16]{0,1:T(8,128)S(1)} %bitcast.101), kind=kOutput, calls=%fused_computation.53 | convolution fusion | flops 1091043328 | bytes 25708544 | tf_op jit(solution)/shard_map/hqk,khd->hqd/dot_general | solution.py:74
  189.0 12.2 %collective-permute-done = bf16[128,1536]{1,0:T(8,128)(2,1)S(1)} collective-permute-done((bf16[128,1536]{1,0:T(8,128)(2,1)S(1)}, bf16[128,1536]{1,0:T(8,128)(2,1)S(1)}, u32[]{:S(2)}, u32[]{:S(2)}) %collective-permute-start) | collective-permute-done | bytes 393248 | tf_op jit(solution)/shard_map/ppermute | solution.py:14
  202.0 8.1 %fusion = f32[128,6144]{1,0:T(8,128)S(1)} fusion(bf16[1,1536,6144]{2,1,0:T(8,128)(2,1)} %param.14, bf16[128,1536]{1,0:T(8,128)(2,1)S(1)} %get-tuple-element.12, f32[1536]{0:T(1024)} %copy-done.4, f32[1536]{0:T(1024)} %copy-done.5, f32[1536]{0:T(1024)S(1)} %get-tuple-element.6, f32[1536]{0:T(1024)S(1)} %get-tuple-element.7, f32[128]{0:T(128)S(1)} %add_rsqrt_fusion.4, ...), kind=kOutput, calls=%fused_computation | convolution fusion | flops 2417688576 | bytes 22439040 | tf_op jit(solution)/shard_map/dot_general | solution.py:51
  210.1 1.5 slice_bitcast_fusion
  211.6 2.5 copy.53
  215.4 2.6 copy.54
  218.0 2.4 multiply_convert_fusion
  221.3 2.0 copy.59
  224.0 1.4 copy.63
  226.3 63.6 %all-gather.9.cloned.1.call-done = bf16[2048,16,128]{2,0,1:T(8,128)(2,1)} async-done(((bf16[128,16,128]{2,0,1:T(8,128)(2,1)}), bf16[2048,16,128]{2,0,1:T(8,128)(2,1)}) %all-gather.9.cloned.1.call-update) | async-done | bytes 8388624 | tf_op jit(solution)/shard_map/all_gather | solution.py:63
  289.9 12.1 %fusion.5 = (f32[16,128]{1,0:T(8,128)S(1)}, f32[16,128,2048]{2,1,0:T(8,128)}) fusion(pred[2048]{0:T(1024)(128)(4,1)S(1)} %iota_compare_fusion, bf16[2048,16,128]{2,0,1:T(8,128)(2,1)} %all-gather.9.cloned.1.call-done, bf16[128,16,128]{2,1,0:T(8,128)(2,1)S(1)} %multiply_convert_fusion.1), kind=kOutput, calls=%fused_computation.9 | convolution fusion | flops 1086322688 | bytes 25700352 | tf_op jit(solution)/shard_map/qhd,khd->hqk/dot_general | solution.py:66
  302.0 7.9 %fusion.8 = f32[16,128]{1,0:T(8,128)S(1)} fusion(f32[16,128,2048]{2,1,0:T(8,128)} %get-tuple-element.23, f32[16,128]{1,0:T(8,128)S(1)} %broadcast_maximum_fusion, pred[2048]{0:T(1024)(128)(4,1)S(1)} %iota_compare_fusion), kind=kLoop, calls=%fused_computation.12 | loop fusion | flops 16775168 | bytes 16795648 | tf_op jit(solution)/shard_map/reduce_sum | solution.py:73
  309.9 56.4 %all-gather.11.cloned.1.call-done = bf16[2048,16,128]{0,2,1:T(8,128)(2,1)} async-done(((bf16[128,16,128]{0,2,1:T(8,128)(2,1)}), bf16[2048,16,128]{0,2,1:T(8,128)(2,1)}) %all-gather.11.cloned.1.call-update) | async-done | bytes 8388624 | tf_op jit(solution)/shard_map/all_gather | solution.py:64
  366.4 10.7 %divide_convert_fusion = bf16[128,16,128]{0,2,1:T(8,128)(2,1)S(1)} fusion(bf16[2048,16,128]{0,2,1:T(8,128)(2,1)} %all-gather.11.cloned.1.call-done, f32[16,128,2048]{2,1,0:T(8,128)} %get-tuple-element.23, f32[16,128]{1,0:T(8,128)S(1)} %broadcast_maximum_fusion, pred[2048]{0:T(1024)(128)(4,1)S(1)} %iota_compare_fusion, f32[128,16]{0,1:T(8,128)S(1)} %bitcast.102), kind=kOutput, calls=%fused_computation.48 | convolution fusion | flops 1091043328 | bytes 25708544 | tf_op jit(solution)/shard_map/hqk,khd->hqd/dot_general | solution.py:74
  378.6 12.2 %collective-permute-done.1 = bf16[128,1536]{1,0:T(8,128)(2,1)S(1)} collective-permute-done((bf16[128,1536]{1,0:T(8,128)(2,1)S(1)}, bf16[128,1536]{1,0:T(8,128)(2,1)S(1)}, u32[]{:S(2)}, u32[]{:S(2)}) %collective-permute-start.1) | collective-permute-done | bytes 393248 | tf_op jit(solution)/shard_map/ppermute | solution.py:14
  (88 shorter events, 14.2 us)
Async XLA Ops:
  6.5 93.4 %all-gather.5.cloned.1.call-start = ((), (), s32[]{:S(2)}) async-start(), calls=%async_computation | async-start | bytes 8912896 | tf_op jit(solution)/shard_map/all_gather | solution.py:63
  7.4 13.1 %copy-start.4 = (f32[1536]{0:T(1024)}, f32[1536]{0:T(1024)S(1)}, u32[]{:S(2)}) copy-start(f32[1536]{0:T(1024)S(1)} %get-tuple-element.9) | copy-start | bytes 18436
  7.4 13.1 %copy-start.5 = (f32[1536]{0:T(1024)}, f32[1536]{0:T(1024)S(1)}, u32[]{:S(2)}) copy-start(f32[1536]{0:T(1024)S(1)} %get-tuple-element.10) | copy-start | bytes 18436
  7.4 179.9 %copy-start.6 = (f32[1536]{0:T(1024)}, f32[1536]{0:T(1024)S(1)}, u32[]{:S(2)}) copy-start(f32[1536]{0:T(1024)S(1)} %get-tuple-element.5) | copy-start | bytes 18436
  7.4 179.9 %copy-start.8 = (f32[1536]{0:T(1024)}, f32[1536]{0:T(1024)S(1)}, u32[]{:S(2)}) copy-start(f32[1536]{0:T(1024)S(1)} %get-tuple-element.8) | copy-start | bytes 18436
  10.5 176.8 %copy-start.10 = (pred[128]{0:T(512)(128)(4,1)}, pred[128]{0:T(512)(128)(4,1)S(1)}, u32[]{:S(2)}) copy-start(pred[128]{0:T(512)(128)(4,1)S(1)} %compare_and_fusion) | copy-start | bytes 388
  10.5 17.9 %copy-start.15 = (s32[9]{0:T(128)S(1)}, s32[9]{0:T(128)}, u32[]{:S(2)}) copy-start(s32[9]{0:T(128)} %param.11) | copy-start | bytes 112
  10.6 19.1 %copy-start.13 = (f32[1,128]{1,0:T(1,128)S(1)}, f32[1,128]{1,0:T(1,128)}, u32[]{:S(2)}) copy-start(f32[1,128]{1,0:T(1,128)} %param.16) | copy-start | bytes 1540
  23.4 153.2 %all-gather.7.cloned.1.call-start = ((), (), s32[]{:S(2)}) async-start(), calls=%async_computation.1 | async-start | bytes 8912896 | tf_op jit(solution)/shard_map/all_gather | solution.py:64
  26.4 263.5 %all-gather.9.cloned.1.call-start = ((), (), s32[]{:S(2)}) async-start(), calls=%async_computation.2 | async-start | bytes 8912896 | tf_op jit(solution)/shard_map/all_gather | solution.py:63
  112.1 75.3 %slice-start = ((s8[6291456]{0:T(1024)(128)(4,1)}), s8[2097152]{0:T(1024)(128)(4,1)S(1)}, s32[]{:S(2)}) async-start(s8[6291456]{0:T(1024)(128)(4,1)} %bitcast.87), calls=%async_computation.4 | async-start | bytes 4194304
  176.6 10.8 %slice-start.1 = ((s8[6291456]{0:T(1024)(128)(4,1)}), s8[4194304]{0:T(1024)(128)(4,1)S(1)}, s32[]{:S(2)}) async-start(s8[6291456]{0:T(1024)(128)(4,1)} %bitcast.87), calls=%async_computation.5 | async-start | bytes 8388608
  176.6 10.8 %copy-start = (bf16[1,128,1536]{2,1,0:T(8,128)(2,1)S(1)}, bf16[1,128,1536]{2,1,0:T(8,128)(2,1)}, u32[]{:S(2)}) copy-start(bf16[1,128,1536]{2,1,0:T(8,128)(2,1)} %param.9) | copy-start | bytes 1179652
  176.6 24.6 %copy-start.3 = (bf16[128,1536]{1,0:T(8,128)(2,1)S(1)}, bf16[128,1536]{1,0:T(8,128)(2,1)}, u32[]{:S(2)}) copy-start(bf16[128,1536]{1,0:T(8,128)(2,1)} %param.10) | copy-start | bytes 1179652
  188.5 12.8 %collective-permute-start = (bf16[128,1536]{1,0:T(8,128)(2,1)S(1)}, bf16[128,1536]{1,0:T(8,128)(2,1)S(1)}, u32[]{:S(2)}, u32[]{:S(2)}) collective-permute-start(bf16[128,1536]{1,0:T(8,128)(2,1)S(1)} %fusion.41), channel_id=1, source_target_pairs={{0,16},{16,32},{32,48},{48,64},{64,80},{80,96},{96,112},{112,0},{1... | collective-permute-start | bytes 1179656 | tf_op jit(solution)/shard_map/ppermute | solution.py:14
  210.0 15.9 %copy-start.14 = (f32[1,128]{1,0:T(1,128)S(1)}, f32[1,128]{1,0:T(1,128)}, u32[]{:S(2)}) copy-start(f32[1,128]{1,0:T(1,128)} %param.16) | copy-start | bytes 1540
  220.4 145.9 %all-gather.11.cloned.1.call-start = ((), (), s32[]{:S(2)}) async-start(), calls=%async_computation.3 | async-start | bytes 8912896 | tf_op jit(solution)/shard_map/all_gather | solution.py:64
  302.0 75.1 %slice-start.2 = ((s8[6291456]{0:T(1024)(128)(4,1)}), s8[2097152]{0:T(1024)(128)(4,1)S(1)}, s32[]{:S(2)}) async-start(s8[6291456]{0:T(1024)(128)(4,1)} %bitcast.89), calls=%async_computation.6 | async-start | bytes 4194304
  366.3 10.8 %slice-start.3 = ((s8[6291456]{0:T(1024)(128)(4,1)}), s8[4194304]{0:T(1024)(128)(4,1)S(1)}, s32[]{:S(2)}) async-start(s8[6291456]{0:T(1024)(128)(4,1)} %bitcast.89), calls=%async_computation.7 | async-start | bytes 8388608
  366.3 10.8 %copy-start.7 = (f32[1536]{0:T(1024)S(1)}, f32[1536]{0:T(1024)}, u32[]{:S(2)}) copy-start(f32[1536]{0:T(1024)} %copy-done.6) | copy-start | bytes 18436
  366.3 10.8 %copy-start.9 = (f32[1536]{0:T(1024)S(1)}, f32[1536]{0:T(1024)}, u32[]{:S(2)}) copy-start(f32[1536]{0:T(1024)} %copy-done.8) | copy-start | bytes 18436
  366.3 10.8 %copy-start.11 = (pred[128]{0:T(512)(128)(4,1)S(1)}, pred[128]{0:T(512)(128)(4,1)}, u32[]{:S(2)}) copy-start(pred[128]{0:T(512)(128)(4,1)} %copy-done.10) | copy-start | bytes 388
  366.4 24.4 %copy-start.2 = (bf16[128,1536]{1,0:T(8,128)(2,1)S(1)}, bf16[128,1536]{1,0:T(8,128)(2,1)}, u32[]{:S(2)}) copy-start(bf16[128,1536]{1,0:T(8,128)(2,1)} %copy-done.1) | copy-start | bytes 1179652
  378.2 12.6 %collective-permute-start.1 = (bf16[128,1536]{1,0:T(8,128)(2,1)S(1)}, bf16[128,1536]{1,0:T(8,128)(2,1)S(1)}, u32[]{:S(2)}, u32[]{:S(2)}) collective-permute-start(bf16[128,1536]{1,0:T(8,128)(2,1)S(1)} %fusion.38), channel_id=1, source_target_pairs={{0,16},{16,32},{32,48},{48,64},{64,80},{80,96},{96,112},{112,0},{1... | collective-permute-start | bytes 1179656 | tf_op jit(solution)/shard_map/ppermute | solution.py:14
  (2 other events, 11.2 us)
Sparse Core Ops, SparseCore 0:
  23.5 76.4 all-gather.4
  102.3 74.2 all-gather.6
  220.5 69.2 all-gather.8
  292.1 74.2 all-gather.10
where the time goes:
time: 399 us; the launch traced here: 398 us
  waiting for transfers between devices  271 us (68%)
  matrix products  64 us (16%)
  other arithmetic  27.4 us (7%)
  local copies, waits for them, and re-layouts  19.3 us (5%)
  between operations  15.4 us (4%)
    all_gather x2, waiting for transfers between devices, run_block(): key_piece = lax.all_gather(key_heads, 'seq', axis=0, tiled=True)  134 us
    all_gather x2, waiting for transfers between devices, run_block(): value_piece = lax.all_gather(value_heads, 'seq', axis=0, tiled=True)  113 us
    ppermute x2, waiting for transfers between devices, from_behind(): return lax.ppermute(value, axis, pairs)  24.5 us
    dot_general x2, matrix products, run_block(): jnp.einsum('qhd,khd->hqk', query_heads, key_piece, preferred_element_type...  24.3 us
    dot_general x2, matrix products, run_block(): jnp.einsum('hqk,khd->hqd', weights.astype(jnp.bfloat16), value_piece, pre...  21.5 us
    dot_general x2, matrix products, run_block(): projected = jnp.dot(mixed_in, w_qkv[0], preferred_element_type=jnp.float32)  16.2 us
    reduce_sum x2, other arithmetic, run_block(): denom = jnp.sum(weights, axis=-1)  15.8 us
  transfers between devices with their start and end apart: 6, of which 6 were waited for; matrix products, arithmetic and copies ran while one was open for 13% of the time, Pallas kernels for 0%

commit v1 on v0

--- a/solution.py
+++ b/solution.py
@@ -60,7 +60,15 @@
         )
         key_limit = text_start + text_live
         row_top = jnp.full((head_count, tok_rows), -1e30, jnp.float32)
-        key_piece = lax.all_gather(key_heads, "seq", axis=0, tiled=True)
+        key_piece = jnp.concatenate(
+            lax.all_to_all(
+                jnp.stack(lax.axis_size("seq") * [key_heads]),
+                axis_name="seq",
+                split_axis=0,
+                concat_axis=0,
+            ),
+            axis=0,
+        )
         value_piece = lax.all_gather(value_heads, "seq", axis=0, tiled=True)
         scores = (
             jnp.einsum("qhd,khd->hqk", query_heads, key_piece, preferred_element_type=jnp.float32)

time: 399 us -> 415 us (1.040)
  local copies, waits for them, and re-layouts: 19.3 us -> 43.5 us
  waiting for transfers between devices: 271 us -> 250 us
  starting transfers between devices: 1.03 us -> 16.6 us
  other arithmetic: 27.4 us -> 23.1 us
    all_to_all x0 -> x2, waiting for transfers between devices: none -> 228 us  [run_block(): lax.all_to_all(jnp.stack(lax.axis_size('seq') * [key_heads]), axis_name='...]
    all_gather x2 -> x0, waiting for transfers between devices: 134 us -> none  [run_block(): key_piece = lax.all_gather(key_heads, 'seq', axis=0, tiled=True)]
    all_gather x2, waiting for transfers between devices: 113 us -> 0.04 us  [run_block(): value_piece = lax.all_gather(value_heads, 'seq', axis=0, tiled=True)]
    all_to_all x0 -> x2, local copies, waits for them, and re-layouts: none -> 20.9 us  [run_block(): lax.all_to_all(jnp.stack(lax.axis_size('seq') * [key_heads]), axis_name='...]
    all_to_all x0 -> x2, starting transfers between devices: none -> 15.5 us  [run_block(): lax.all_to_all(jnp.stack(lax.axis_size('seq') * [key_heads]), axis_name='...]
    another operation x0 -> x2, local copies, waits for them, and re-layouts: none -> 10.8 us  [run_block(): jnp.stack(lax.axis_size('seq') * [key_heads])]
  transfers between devices with their start and end apart: 6 -> 6, of which waited for: 6 -> 4; matrix products, arithmetic and copies ran while one was open for 13% -> 19% of each run, Pallas kernels for 0% -> 0%
where the time goes in v1:
time: 415 us; the launch traced here: 412 us
  waiting for transfers between devices  250 us (60%)
  matrix products  63.3 us (15%)
  local copies, waits for them, and re-layouts  43.5 us (10%)
  other arithmetic  23.1 us (6%)
  starting transfers between devices  16.6 us (4%)
  between operations  15.9 us (4%)
    all_to_all x2, waiting for transfers between devices, run_block(): lax.all_to_all(jnp.stack(lax.axis_size('seq') * [key_heads]), axis_name='...  228 us
    dot_general x2, matrix products, run_block(): jnp.einsum('qhd,khd->hqk', query_heads, key_piece, preferred_element_type...  23.5 us
    ppermute x2, waiting for transfers between devices, from_behind(): return lax.ppermute(value, axis, pairs)  22 us
    dot_general x2, matrix products, run_block(): jnp.einsum('hqk,khd->hqd', weights.astype(jnp.bfloat16), value_piece, pre...  21.5 us
    all_to_all x2, local copies, waits for them, and re-layouts, run_block(): lax.all_to_all(jnp.stack(lax.axis_size('seq') * [key_heads]), axis_name='...  20.9 us
    dot_general x2, matrix products, run_block(): projected = jnp.dot(mixed_in, w_qkv[0], preferred_element_type=jnp.float32)  16.2 us
    reduce_sum x2, other arithmetic, run_block(): denom = jnp.sum(weights, axis=-1)  15.8 us
    all_to_all x2, starting transfers between devices, run_block(): lax.all_to_all(jnp.stack(lax.axis_size('seq') * [key_heads]), axis_name='...  15.5 us
  transfers between devices with their start and end apart: 6, of which 4 were waited for; matrix products, arithmetic and copies ran while one was open for 19% of the time, Pallas kernels for 0%

profile of v1, /device:TPU:1, one launch (start us, length us, event | category | flops | bytes accessed | tf_op | source)
XLA Modules:
  0.0 412.2 jit_solution(4787157469805798683)
XLA Ops:
  8.1 1.1 convert_reduce_fusion.1
  9.2 1.2 fusion.62
  10.5 8.1 %fusion.2 = f32[128,6144]{1,0:T(8,128)S(1)} fusion(bf16[1,1536,6144]{2,1,0:T(8,128)(2,1)} %param.14, bf16[1,128,1536]{2,1,0:T(8,128)(2,1)} %param.9, f32[1536]{0:T(1024)S(1)} %get-tuple-element.9, f32[1536]{0:T(1024)S(1)} %get-tuple-element.10, f32[1536]{0:T(1024)S(1)} %get-tuple-element.6, f32[1536]{0:T(1024)S(1)} %get-tuple-element.7, ...), kind=kOutput, calls=%fused_computation.2 | convolution fusion | flops 2417688576 | bytes 22439040 | tf_op jit(solution)/shard_map/dot_general | solution.py:51
  19.6 2.0 copy.45
  21.6 1.2 slice_bitcast_fusion.3
  24.1 5.4 %stack.10 = bf16[16,128,16,128]{3,1,2,0:T(8,128)(2,1)} broadcast(bf16[128,16,128]{2,0,1:T(8,128)(2,1)S(1)} %copy.32), dimensions={1,2,3} | broadcast | bytes 8912896 | tf_op jit(solution)/shard_map/stack | solution.py:65
  29.6 9.3 %all-to-all-start = ((bf16[16,128,16,128]{3,1,2,0:T(8,128)(2,1)}), bf16[16,128,16,128]{3,1,2,0:T(8,128)(2,1)}, u32[]{:S(2)}, u32[]{:S(2)}) async-start(bf16[16,128,16,128]{3,1,2,0:T(8,128)(2,1)} %stack.10), calls=%async_computation | async-start | bytes 16777216 | tf_op jit(solution)/shard_map/all_to_all | solution.py:64
  41.5 118.5 %all-to-all-done = bf16[16,128,16,128]{3,1,2,0:T(8,128)(2,1)} async-done(((bf16[16,128,16,128]{3,1,2,0:T(8,128)(2,1)}), bf16[16,128,16,128]{3,1,2,0:T(8,128)(2,1)}, u32[]{:S(2)}, u32[]{:S(2)}) %all-to-all-start) | async-done | bytes 8388640 | tf_op jit(solution)/shard_map/all_to_all | solution.py:64
  159.9 10.5 %copy.33 = bf16[16,128,16,128]{3,1,0,2:T(8,128)(2,1)} copy(bf16[16,128,16,128]{3,1,2,0:T(8,128)(2,1)} %all-to-all-done) | data formatting | bytes 16777216 | tf_op jit(solution)/shard_map/all_to_all | solution.py:64
  170.5 11.8 %fusion.4 = (f32[16,128]{1,0:T(8,128)S(1)}, f32[16,128,2048]{2,1,0:T(8,128)}) fusion(pred[2048]{0:T(1024)(128)(4,1)S(1)} %iota_compare_fusion.1, bf16[2048,16,128]{2,0,1:T(8,128)(2,1)} %bitcast.84, bf16[128,16,128]{2,1,0:T(8,128)(2,1)S(1)} %multiply_convert_fusion.3), kind=kOutput, calls=%fused_computation.8 | convolution fusion | flops 1086322688 | bytes 25700352 | tf_op jit(solution)/shard_map/qhd,khd->hqk/dot_general | solution.py:74
  182.2 7.9 %fusion.6 = f32[16,128]{1,0:T(8,128)S(1)} fusion(f32[16,128,2048]{2,1,0:T(8,128)} %get-tuple-element.20, f32[16,128]{1,0:T(8,128)S(1)} %broadcast_maximum_fusion.1, pred[2048]{0:T(1024)(128)(4,1)S(1)} %iota_compare_fusion.1), kind=kLoop, calls=%fused_computation.10 | loop fusion | flops 16775168 | bytes 16795648 | tf_op jit(solution)/shard_map/reduce_sum | solution.py:81
  190.2 10.7 %divide_convert_fusion.1 = bf16[128,16,128]{0,2,1:T(8,128)(2,1)S(1)} fusion(bf16[2048,16,128]{0,2,1:T(8,128)(2,1)} %all-gather.3.cloned.1.call-done, f32[16,128,2048]{2,1,0:T(8,128)} %get-tuple-element.20, f32[16,128]{1,0:T(8,128)S(1)} %broadcast_maximum_fusion.1, pred[2048]{0:T(1024)(128)(4,1)S(1)} %iota_compare_fusion.1, f32[128,16]{0,1:T(8,128)S(1)} %bitcast.100), kind=kOutput, calls=%fused_computation.52 | convolution fusion | flops 1091043328 | bytes 25708544 | tf_op jit(solution)/shard_map/hqk,khd->hqd/dot_general | solution.py:82
  202.9 11.4 %collective-permute-done = bf16[128,1536]{1,0:T(8,128)(2,1)S(1)} collective-permute-done((bf16[128,1536]{1,0:T(8,128)(2,1)S(1)}, bf16[128,1536]{1,0:T(8,128)(2,1)S(1)}, u32[]{:S(2)}, u32[]{:S(2)}) %collective-permute-start) | collective-permute-done | bytes 393248 | tf_op jit(solution)/shard_map/ppermute | solution.py:14
  215.0 8.1 %fusion = f32[128,6144]{1,0:T(8,128)S(1)} fusion(bf16[1,1536,6144]{2,1,0:T(8,128)(2,1)} %param.14, bf16[128,1536]{1,0:T(8,128)(2,1)S(1)} %get-tuple-element.12, f32[1536]{0:T(1024)} %copy-done.6, f32[1536]{0:T(1024)} %copy-done.7, f32[1536]{0:T(1024)S(1)} %get-tuple-element.6, f32[1536]{0:T(1024)S(1)} %get-tuple-element.7, f32[128]{0:T(128)S(1)} %add_rsqrt_fusion.4, ...), kind=kOutput, calls=%fused_computation | convolution fusion | flops 2417688576 | bytes 22439040 | tf_op jit(solution)/shard_map/dot_general | solution.py:51
  223.9 2.0 copy.46
  226.0 1.2 slice_bitcast_fusion.1
  229.1 5.3 %stack.12 = bf16[16,128,16,128]{3,1,2,0:T(8,128)(2,1)} broadcast(bf16[128,16,128]{2,0,1:T(8,128)(2,1)S(1)} %copy.40), dimensions={1,2,3} | broadcast | bytes 8912896 | tf_op jit(solution)/shard_map/stack | solution.py:65
  234.5 6.3 %all-to-all-start.1 = ((bf16[16,128,16,128]{3,1,2,0:T(8,128)(2,1)}), bf16[16,128,16,128]{3,1,2,0:T(8,128)(2,1)}, u32[]{:S(2)}, u32[]{:S(2)}) async-start(bf16[16,128,16,128]{3,1,2,0:T(8,128)(2,1)} %stack.12), calls=%async_computation.1 | async-start | bytes 16777216 | tf_op jit(solution)/shard_map/all_to_all | solution.py:64
  242.4 109.3 %all-to-all-done.1 = bf16[16,128,16,128]{3,1,2,0:T(8,128)(2,1)} async-done(((bf16[16,128,16,128]{3,1,2,0:T(8,128)(2,1)}), bf16[16,128,16,128]{3,1,2,0:T(8,128)(2,1)}, u32[]{:S(2)}, u32[]{:S(2)}) %all-to-all-start.1) | async-done | bytes 8388640 | tf_op jit(solution)/shard_map/all_to_all | solution.py:64
  351.7 10.3 %copy.41 = bf16[16,128,16,128]{3,1,0,2:T(8,128)(2,1)} copy(bf16[16,128,16,128]{3,1,2,0:T(8,128)(2,1)} %all-to-all-done.1) | data formatting | bytes 16777216 | tf_op jit(solution)/shard_map/all_to_all | solution.py:64
  362.1 11.8 %fusion.5 = (f32[16,128]{1,0:T(8,128)S(1)}, f32[16,128,2048]{2,1,0:T(8,128)}) fusion(pred[2048]{0:T(1024)(128)(4,1)S(1)} %iota_compare_fusion, bf16[2048,16,128]{2,0,1:T(8,128)(2,1)} %bitcast.85, bf16[128,16,128]{2,1,0:T(8,128)(2,1)S(1)} %multiply_convert_fusion.1), kind=kOutput, calls=%fused_computation.9 | convolution fusion | flops 1086322688 | bytes 25700352 | tf_op jit(solution)/shard_map/qhd,khd->hqk/dot_general | solution.py:74
  373.9 7.9 %fusion.8 = f32[16,128]{1,0:T(8,128)S(1)} fusion(f32[16,128,2048]{2,1,0:T(8,128)} %get-tuple-element.22, f32[16,128]{1,0:T(8,128)S(1)} %broadcast_maximum_fusion, pred[2048]{0:T(1024)(128)(4,1)S(1)} %iota_compare_fusion), kind=kLoop, calls=%fused_computation.12 | loop fusion | flops 16775168 | bytes 16795648 | tf_op jit(solution)/shard_map/reduce_sum | solution.py:81
  381.9 10.7 %divide_convert_fusion = bf16[128,16,128]{0,2,1:T(8,128)(2,1)S(1)} fusion(bf16[2048,16,128]{0,2,1:T(8,128)(2,1)} %all-gather.5.cloned.1.call-done, f32[16,128,2048]{2,1,0:T(8,128)} %get-tuple-element.22, f32[16,128]{1,0:T(8,128)S(1)} %broadcast_maximum_fusion, pred[2048]{0:T(1024)(128)(4,1)S(1)} %iota_compare_fusion, f32[128,16]{0,1:T(8,128)S(1)} %bitcast.101), kind=kOutput, calls=%fused_computation.47 | convolution fusion | flops 1091043328 | bytes 25708544 | tf_op jit(solution)/shard_map/hqk,khd->hqd/dot_general | solution.py:82
  393.8 10.6 %collective-permute-done.1 = bf16[128,1536]{1,0:T(8,128)(2,1)S(1)} collective-permute-done((bf16[128,1536]{1,0:T(8,128)(2,1)S(1)}, bf16[128,1536]{1,0:T(8,128)(2,1)S(1)}, u32[]{:S(2)}, u32[]{:S(2)}) %collective-permute-start.1) | collective-permute-done | bytes 393248 | tf_op jit(solution)/shard_map/ppermute | solution.py:14
  (98 shorter events, 13.4 us)
Async XLA Ops:
  6.5 183.6 %all-gather.3.cloned.1.call-start = ((), (), s32[]{:S(2)}) async-start(), calls=%async_computation.2 | async-start | bytes 8912896 | tf_op jit(solution)/shard_map/all_gather | solution.py:72
  7.4 15.6 %copy-start.6 = (f32[1536]{0:T(1024)}, f32[1536]{0:T(1024)S(1)}, u32[]{:S(2)}) copy-start(f32[1536]{0:T(1024)S(1)} %get-tuple-element.9) | copy-start | bytes 18436
  7.4 15.6 %copy-start.7 = (f32[1536]{0:T(1024)}, f32[1536]{0:T(1024)S(1)}, u32[]{:S(2)}) copy-start(f32[1536]{0:T(1024)S(1)} %get-tuple-element.10) | copy-start | bytes 18436
  7.4 193.5 %copy-start.8 = (f32[1536]{0:T(1024)}, f32[1536]{0:T(1024)S(1)}, u32[]{:S(2)}) copy-start(f32[1536]{0:T(1024)S(1)} %get-tuple-element.5) | copy-start | bytes 18436
  7.4 193.5 %copy-start.10 = (f32[1536]{0:T(1024)}, f32[1536]{0:T(1024)S(1)}, u32[]{:S(2)}) copy-start(f32[1536]{0:T(1024)S(1)} %get-tuple-element.8) | copy-start | bytes 18436
  10.5 190.4 %copy-start.12 = (pred[128]{0:T(512)(128)(4,1)}, pred[128]{0:T(512)(128)(4,1)S(1)}, u32[]{:S(2)}) copy-start(pred[128]{0:T(512)(128)(4,1)S(1)} %compare_and_fusion) | copy-start | bytes 388
  10.5 13.1 %copy-start.14 = (f32[1,128]{1,0:T(1,128)S(1)}, f32[1,128]{1,0:T(1,128)}, u32[]{:S(2)}) copy-start(f32[1,128]{1,0:T(1,128)} %param.17) | copy-start | bytes 1540
  22.9 16.2 %copy-start.1 = (f32[16,8,16,128]{3,1,2,0:T(8,128)S(1)}, f32[16,8,16,128]{3,1,2,0:T(8,128)}, u32[]{:S(2)}) copy-start(f32[16,8,16,128]{3,1,2,0:T(8,128)} %get-tuple-element.15) | copy-start | bytes 3145732
  23.1 16.8 %copy-start.17 = (s32[9]{0:T(128)S(1)}, s32[9]{0:T(128)}, u32[]{:S(2)}) copy-start(s32[9]{0:T(128)} %param.11) | copy-start | bytes 112
  23.1 18.0 %copy-start.15 = (f32[1,128]{1,0:T(1,128)S(1)}, f32[1,128]{1,0:T(1,128)}, u32[]{:S(2)}) copy-start(f32[1,128]{1,0:T(1,128)} %param.16) | copy-start | bytes 1540
  29.6 130.4 %all-to-all-start = ((bf16[16,128,16,128]{3,1,2,0:T(8,128)(2,1)}), bf16[16,128,16,128]{3,1,2,0:T(8,128)(2,1)}, u32[]{:S(2)}, u32[]{:S(2)}) async-start(bf16[16,128,16,128]{3,1,2,0:T(8,128)(2,1)} %stack.10), calls=%async_computation | async-start | bytes 16777216 | tf_op jit(solution)/shard_map/all_to_all | solution.py:64
  38.8 343.0 %all-gather.5.cloned.1.call-start = ((), (), s32[]{:S(2)}) async-start(), calls=%async_computation.3 | async-start | bytes 8912896 | tf_op jit(solution)/shard_map/all_gather | solution.py:72
  182.2 18.8 %slice-start = ((s8[6291456]{0:T(1024)(128)(4,1)}), s8[2097152]{0:T(1024)(128)(4,1)S(1)}, s32[]{:S(2)}) async-start(s8[6291456]{0:T(1024)(128)(4,1)} %bitcast.86), calls=%async_computation.4 | async-start | bytes 4194304
  190.2 10.8 %slice-start.1 = ((s8[6291456]{0:T(1024)(128)(4,1)}), s8[4194304]{0:T(1024)(128)(4,1)S(1)}, s32[]{:S(2)}) async-start(s8[6291456]{0:T(1024)(128)(4,1)} %bitcast.86), calls=%async_computation.5 | async-start | bytes 8388608
  190.2 10.8 %copy-start = (bf16[1,128,1536]{2,1,0:T(8,128)(2,1)S(1)}, bf16[1,128,1536]{2,1,0:T(8,128)(2,1)}, u32[]{:S(2)}) copy-start(bf16[1,128,1536]{2,1,0:T(8,128)(2,1)} %param.9) | copy-start | bytes 1179652
  190.2 24.1 %copy-start.5 = (bf16[128,1536]{1,0:T(8,128)(2,1)S(1)}, bf16[128,1536]{1,0:T(8,128)(2,1)}, u32[]{:S(2)}) copy-start(bf16[128,1536]{1,0:T(8,128)(2,1)} %param.10) | copy-start | bytes 1179652
  202.0 12.2 %collective-permute-start = (bf16[128,1536]{1,0:T(8,128)(2,1)S(1)}, bf16[128,1536]{1,0:T(8,128)(2,1)S(1)}, u32[]{:S(2)}, u32[]{:S(2)}) collective-permute-start(bf16[128,1536]{1,0:T(8,128)(2,1)S(1)} %fusion.41), channel_id=1, source_target_pairs={{0,16},{16,32},{32,48},{48,64},{64,80},{80,96},{96,112},{112,0},{1... | collective-permute-start | bytes 1179656 | tf_op jit(solution)/shard_map/ppermute | solution.py:14
  227.2 14.1 %copy-start.2 = (f32[16,8,16,128]{3,1,2,0:T(8,128)S(1)}, f32[16,8,16,128]{3,1,2,0:T(8,128)}, u32[]{:S(2)}) copy-start(f32[16,8,16,128]{3,1,2,0:T(8,128)} %get-tuple-element.13) | copy-start | bytes 3145732
  227.4 14.6 %copy-start.16 = (f32[1,128]{1,0:T(1,128)S(1)}, f32[1,128]{1,0:T(1,128)}, u32[]{:S(2)}) copy-start(f32[1,128]{1,0:T(1,128)} %param.16) | copy-start | bytes 1540
  234.5 117.3 %all-to-all-start.1 = ((bf16[16,128,16,128]{3,1,2,0:T(8,128)(2,1)}), bf16[16,128,16,128]{3,1,2,0:T(8,128)(2,1)}, u32[]{:S(2)}, u32[]{:S(2)}) async-start(bf16[16,128,16,128]{3,1,2,0:T(8,128)(2,1)} %stack.12), calls=%async_computation.1 | async-start | bytes 16777216 | tf_op jit(solution)/shard_map/all_to_all | solution.py:64
  373.9 18.7 %slice-start.2 = ((s8[6291456]{0:T(1024)(128)(4,1)}), s8[2097152]{0:T(1024)(128)(4,1)S(1)}, s32[]{:S(2)}) async-start(s8[6291456]{0:T(1024)(128)(4,1)} %bitcast.88), calls=%async_computation.6 | async-start | bytes 4194304
  381.8 10.8 %slice-start.3 = ((s8[6291456]{0:T(1024)(128)(4,1)}), s8[4194304]{0:T(1024)(128)(4,1)S(1)}, s32[]{:S(2)}) async-start(s8[6291456]{0:T(1024)(128)(4,1)} %bitcast.88), calls=%async_computation.7 | async-start | bytes 8388608
  381.8 22.6 %copy-start.4 = (bf16[128,1536]{1,0:T(8,128)(2,1)S(1)}, bf16[128,1536]{1,0:T(8,128)(2,1)}, u32[]{:S(2)}) copy-start(bf16[128,1536]{1,0:T(8,128)(2,1)} %copy-done.3) | copy-start | bytes 1179652
  393.7 10.7 %collective-permute-start.1 = (bf16[128,1536]{1,0:T(8,128)(2,1)S(1)}, bf16[128,1536]{1,0:T(8,128)(2,1)S(1)}, u32[]{:S(2)}, u32[]{:S(2)}) collective-permute-start(bf16[128,1536]{1,0:T(8,128)(2,1)S(1)} %fusion.38), channel_id=1, source_target_pairs={{0,16},{16,32},{32,48},{48,64},{64,80},{80,96},{96,112},{112,0},{1... | collective-permute-start | bytes 1179656 | tf_op jit(solution)/shard_map/ppermute | solution.py:14
  (4 other events, 33.2 us)
Sparse Core Ops, SparseCore 0:
  21.7 150.0 all-gather.2
  226.1 145.7 all-gather.4
